TPU v7x, 32 devices: a whole 2x2x4 slice. The times are simulated.
32 devices in a mesh: groups: 2 (over y), view: 4 (over z), row: 4 (over x, core).
Axes of the slice: x: 2, y: 2, z: 4, core: 2. Of those that a mesh axis runs over, the one named last changes fastest.
Arguments:
- inputs: bfloat16 [64, 292, 16, 16], P(None, 'view', ('groups', 'row')), parts along dimension 2, may hold values from -24 to 24
- cotangent: bfloat16 [64, 292, 16, 16], P(None, None, ('groups', 'row'), 'view'), parts along dimension 2, may hold values from -6 to 6
- keep: int32 [584], P('groups'), parts along dimension 0, may hold values from 0 to 1, as said below
- w_conv: bfloat16 [64, 64, 3, 3], replicated, may hold values from -0.25 to 0.25
- gain: float32 [64], replicated, may hold values from 0.5 to 1.5
- w_query: bfloat16 [64, 64], replicated, may hold values from -3 to 3
- w_key: bfloat16 [64, 64], replicated, may hold values from -3 to 3
- w_value: bfloat16 [64, 64], replicated, may hold values from -0.75 to 0.75
- w_out: bfloat16 [64, 64], replicated, may hold values from -0.75 to 0.75
Outputs:
- output: bfloat16 [64, 292, 16, 16], P(None, None, ('groups', 'row'), 'view'), parts along dimension 2
- d_input: bfloat16 [64, 292, 16, 16], P(None, 'view', ('groups', 'row')), parts along dimension 2
- g_conv: float32 [128, 64, 3, 3], P('groups'), parts along dimension 0
- g_gain: float32 [128], P('groups'), parts along dimension 0
- g_query: float32 [128, 64], P('groups'), parts along dimension 0
- g_key: float32 [128, 64], P('groups'), parts along dimension 0
- g_value: float32 [128, 64], P('groups'), parts along dimension 0
- g_out: float32 [128, 64], P('groups'), parts along dimension 0
There are 2 independent parts, one for each index of `groups`. A program takes and returns all parts, laid end to end along the dimension named above; an argument that names none is the same for every part. Nothing has to cross between parts.
Inputs may be any that keep to these rules, and one draw needn't show every extreme that they name: `keep`: zero at every view from 289 on, one at view 289 // 2.
All inputs are finite; a program needn't handle non-finite values.
Results may differ from a plain program's by a relative error of at most 0.012.
The roundings to bfloat16 on the way count: a program that leaves them out, or rounds other values in their place, can miss the bound.
Values may be sent and summed in bfloat16 or wider, within the bound.
No kernel may reach another device: no remote copies, remote signals or barrier semaphores. Data moves between devices by JAX's collectives and lax.ppermute only.
A program may use at most 64 MiB of HBM per device.

v0:
```python
import math
import jax
import jax.numpy as jnp
from jax import lax
from jax.sharding import PartitionSpec as P


def with_halo(cells, sides, width):
    for axis, dim in sides:
        count = lax.axis_size(axis)
        ends = count - 1
        head = lax.slice_in_dim(cells, 0, width, axis=dim)
        tail = lax.slice_in_dim(cells, cells.shape[dim] - width, cells.shape[dim], axis=dim)
        cells = jnp.concatenate(
            [
                lax.ppermute(tail, axis, [(i, (i + 1) % count) for i in range(ends)]),
                cells,
                lax.ppermute(head, axis, [((i + 1) % count, i) for i in range(ends)]),
            ],
            axis=dim,
        )
    return cells


def product(form, left, right):
    return jnp.einsum(form, left, right, preferred_element_type=jnp.float32)


def convolve(padded, w_conv):
    height = padded.shape[2] - 2
    breadth = padded.shape[3] - 2
    total = jnp.zeros((w_conv.shape[0], padded.shape[1], height, breadth), jnp.float32)
    for row_tap in range(3):
        for col_tap in range(3):
            window = padded[:, :, row_tap : row_tap + height, col_tap : col_tap + breadth]
            total = total + product("oc,cvrw->ovrw", w_conv[:, :, row_tap, col_tap], window)
    return total


def input_grad(grad_pad, w_conv):
    height = grad_pad.shape[2] - 2
    breadth = grad_pad.shape[3] - 2
    total = jnp.zeros((w_conv.shape[1], grad_pad.shape[1], height, breadth), jnp.float32)
    for row_tap in range(3):
        for col_tap in range(3):
            window = grad_pad[
                :, :, 2 - row_tap : 2 - row_tap + height, 2 - col_tap : 2 - col_tap + breadth
            ]
            total = total + product("oc,ovrw->cvrw", w_conv[:, :, row_tap, col_tap], window)
    return total


def weight_grad(grad, padded):
    height = grad.shape[2]
    breadth = grad.shape[3]
    taps = []
    for row_tap in range(3):
        for col_tap in range(3):
            window = padded[:, :, row_tap : row_tap + height, col_tap : col_tap + breadth]
            taps.append(product("ovrw,cvrw->oc", grad, window))
    stacked = jnp.stack(taps, axis=2)
    return stacked.reshape(grad.shape[0], padded.shape[0], 3, 3)


def angular(mixed_in, grad_out, keep, gain, w_query, w_key, w_value, w_out, used):
    pixels, all_views, channels = mixed_in.shape
    scale = 1.0 / math.sqrt(channels)
    values = mixed_in.astype(jnp.float32)
    centred = values - jnp.mean(values, axis=2, keepdims=True)
    rstd = lax.rsqrt(jnp.mean(centred * centred, axis=2, keepdims=True) + 1e-05)
    normed = centred * rstd
    normal_in = (normed * gain[None, None, :]).astype(jnp.bfloat16)
    query = product("cd,pvc->pvd", w_query, normal_in).astype(jnp.bfloat16)
    key_proj = product("cd,pvc->pvd", w_key, normal_in).astype(jnp.bfloat16)
    value_proj = product("cd,pvc->pvd", w_value, normal_in).astype(jnp.bfloat16)
    scores = product("pvd,pud->pvu", query, key_proj) * scale
    scores = jnp.where(keep[None, None, :used] > 0, scores, -1e30)
    highest = jnp.max(scores, axis=2, keepdims=True)
    expo = jnp.exp(scores - highest)
    probs = expo / jnp.sum(expo, axis=2, keepdims=True)
    probs_b = probs.astype(jnp.bfloat16)
    attended = product("pvu,pud->pvd", probs_b, value_proj).astype(jnp.bfloat16)
    output = (values + product("dc,pvd->pvc", w_out, attended)).astype(jnp.bfloat16)
    d_attended = product("dc,pvc->pvd", w_out, grad_out).astype(jnp.bfloat16)
    g_out = product("pvd,pvc->dc", attended, grad_out)
    d_probs = product("pvd,pud->pvu", d_attended, value_proj)
    d_value = product("pvu,pvd->pud", probs_b, d_attended).astype(jnp.bfloat16)
    inner = jnp.sum(probs * d_probs, axis=2, keepdims=True)
    d_scores = (probs * (d_probs - inner) * scale).astype(jnp.bfloat16)
    d_query = product("pvu,pud->pvd", d_scores, key_proj).astype(jnp.bfloat16)
    d_key = product("pvu,pvd->pud", d_scores, query).astype(jnp.bfloat16)
    g_query = product("pvc,pvd->cd", normal_in, d_query)
    g_key = product("pvc,pvd->cd", normal_in, d_key)
    g_value = product("pvc,pvd->cd", normal_in, d_value)
    d_normal = (
        product("cd,pvd->pvc", w_query, d_query)
        + product("cd,pvd->pvc", w_key, d_key)
        + product("cd,pvd->pvc", w_value, d_value)
    )
    g_gain = jnp.sum(d_normal * normed, axis=(0, 1))
    scaled = d_normal * gain[None, None, :]
    back = (
        scaled
        - jnp.mean(scaled, axis=2, keepdims=True)
        - normed * jnp.mean(scaled * normed, axis=2, keepdims=True)
    )
    d_spatial = (grad_out.astype(jnp.float32) + back * rstd).astype(jnp.bfloat16)
    return (output, d_spatial, (g_gain, g_query, g_key, g_value, g_out))


def angular_rows(spatial, cotangent, keep, gain, w_query, w_key, w_value, w_out, used):

    def row_pass(pair):
        return angular(pair[0], pair[1], keep, gain, w_query, w_key, w_value, w_out, used)

    spatial_last = jnp.transpose(spatial, (2, 3, 1, 0))
    cotangent_last = jnp.transpose(cotangent, (2, 3, 1, 0))
    out_rows, grad_rows, grads = lax.map(row_pass, (spatial_last, cotangent_last))
    summed = tuple((jnp.sum(item, axis=0) for item in grads))
    return (jnp.transpose(out_rows, (3, 2, 0, 1)), jnp.transpose(grad_rows, (3, 2, 0, 1)), summed)


def body(inputs, cotangent, keep, w_conv, gain, w_query, w_key, w_value, w_out):
    channels, view_dev, row_dev, width = inputs.shape
    blocks = lax.axis_size("view")
    breadth = width // blocks
    all_views = view_dev * blocks
    padded = with_halo(inputs, (("row", 2),), 1)
    padded = jnp.pad(padded, ((0, 0), (0, 0), (0, 0), (1, 1)))
    spatial = (inputs.astype(jnp.float32) + convolve(padded, w_conv)).astype(jnp.bfloat16)
    moved = lax.all_to_all(
        spatial.reshape(channels, view_dev, row_dev, blocks, breadth),
        "view",
        split_axis=3,
        concat_axis=1,
        tiled=True,
    )
    moved = moved.reshape(channels, all_views, row_dev, breadth)
    output, d_spatial, grads = angular_rows(
        moved, cotangent, keep, gain, w_query, w_key, w_value, w_out, all_views
    )
    returned = lax.all_to_all(
        d_spatial.reshape(channels, all_views, row_dev, 1, breadth),
        "view",
        split_axis=1,
        concat_axis=3,
        tiled=True,
    )
    returned = returned.reshape(channels, view_dev, row_dev, width)
    grad_pad = with_halo(returned, (("row", 2),), 1)
    grad_pad = jnp.pad(grad_pad, ((0, 0), (0, 0), (0, 0), (1, 1)))
    d_input = (returned.astype(jnp.float32) + input_grad(grad_pad, w_conv)).astype(jnp.bfloat16)
    g_conv = weight_grad(returned, padded)
    g_gain, g_query, g_key, g_value, g_out = grads
    g_conv, g_gain, g_query, g_key, g_value, g_out = lax.psum(
        (g_conv, g_gain, g_query, g_key, g_value, g_out), ("view", "row")
    )
    return (output, d_input, g_conv, g_gain, g_query, g_key, g_value, g_out)


def solution(mesh):
    placed = (
        P(None, "view", ("groups", "row"), None),
        P(None, None, ("groups", "row"), "view"),
        P("groups"),
        P(),
        P(),
        P(),
        P(),
        P(),
        P(),
    )
    return jax.shard_map(
        body,
        mesh=mesh,
        in_specs=placed,
        out_specs=(
            P(None, None, ("groups", "row"), "view"),
            P(None, "view", ("groups", "row"), None),
            P("groups", None, None, None),
            P("groups"),
            P("groups", None),
            P("groups", None),
            P("groups", None),
            P("groups", None),
        ),
        check_vma=False,
    )
```

profile of v0, /device:TPU:0, one launch (start us, length us, event | category | flops | bytes accessed | tf_op | source)
XLA Modules:
  0.0 311.2 jit_solution(1073874773569292355)
XLA Ops:
  8.4 2.4 collective-permute-start
  13.2 3.2 %collective-permute-done.1 = bf16[64,73,1,16]{1,0,3,2:T(8,128)(2,1)S(1)} collective-permute-done((bf16[64,73,1,16]{1,0,3,2:T(8,128)(2,1)S(1)}, bf16[64,73,1,16]{1,0,3,2:T(8,128)(2,1)S(1)}, u32[]{:S(2)}, u32[]{:S(2)}) %collective-permute-start.1) | collective-permute-done | bytes 149536 | tf_op jit(solution)/shard_map/ppermute | solution.py:18
  20.0 5.0 %all-to-all-start = ((bf16[64,73,2,4,4]{1,0,4,2,3:T(8,128)(2,1)}), bf16[64,73,2,4,4]{1,0,4,2,3:T(8,128)(2,1)S(1)}, u32[]{:S(2)}, u32[]{:S(2)}) async-start(bf16[64,73,2,4,4]{1,0,4,2,3:T(8,128)(2,1)} %copy.93), calls=%async_computation | async-start | bytes 1048576 | tf_op jit(solution)/shard_map/all_to_all | solution.py:131
  25.1 12.3 %all-to-all-done = bf16[64,73,2,4,4]{1,0,4,2,3:T(8,128)(2,1)S(1)} async-done(((bf16[64,73,2,4,4]{1,0,4,2,3:T(8,128)(2,1)}), bf16[64,73,2,4,4]{1,0,4,2,3:T(8,128)(2,1)S(1)}, u32[]{:S(2)}, u32[]{:S(2)}) %all-to-all-start) | async-done | bytes 299040 | tf_op jit(solution)/shard_map/all_to_all | solution.py:131
  38.2 56.6 %while.22 = (s32[]{:T(128)}, bf16[2,4,292,64]{2,1,0,3:T(4,128)(2,1)}, bf16[2,4,292,64]{2,3,1,0:T(8,128)(2,1)}, f32[2,64]{1,0:T(2,128)}, f32[2,64,64]{2,1,0:T(8,1...) while((s32[]{:T(128)}, ...), condition=%wide.region_9.10_spmd, body=%wide.region_0.9_spmd.sunk | while | flops 399432576 | bytes 35407752 | solution.py:118
  41.3 1.6 convolution_convert_fusion.12
  42.9 3.1 %fusion.288 = (f32[4,292]{1,0:T(4,128)S(1)}, f32[4,292,292]{1,2,0:T(8,128)}) fusion(pred[292]{0:T(512)(128)(4,1)S(1)} %broadcast_compare_fusion.2, bf16[4,292,64]{1,2,0:T(8,128)(2,1)} %convolution_convert_fusion.12, bf16[64,64]{1,0:T(8,128)(2,1)S(1)} %copy-done.17, f32[64]{0:T(128)} %get-tuple-element.425, f32[4,292]{1,0:T(4,128)S(1)} %add_rsqrt_fusion.2, ...), kind=kOutput, calls=%fused_computation.193.clone.1 | convolution fusion | flops 55036452 | bytes 1744452 | tf_op jit(solution)/shard_map/while/body/eval_jaxpr/sub | solution.py:79
  46.0 3.5 %fusion.293 = bf16[4,292,64]{1,2,0:T(8,128)(2,1)} fusion(f32[4,292,292]{1,2,0:T(8,128)S(1)} %fusion.290, f32[4,292,292]{1,2,0:T(8,128)} %get-tuple-element.288, f32[4,292]{1,0:T(4,128)S(1)} %get-tuple-element.289, bf16[64,64]{1,0:T(8,128)(2,1)S(1)} %copy-done.17, f32[64]{0:T(128)} %get-tuple-element.425, f32[4,292]{1,0:T(4,128)S(1)} %add_rsqrt_fusion.2, ...), kind=kOutput, calls=%fused_computation.14.clone.1 | convolution fusion | flops 56135540 | bytes 7662592 | tf_op jit(solution)/shard_map/while/body/eval_jaxpr/pvu,pvd->pud/dot_general | solution.py:26
  49.6 3.5 %fusion.291 = bf16[4,292,64]{1,2,0:T(8,128)(2,1)} fusion(bf16[4,292,64]{1,2,0:T(8,128)(2,1)} %convolution_convert_fusion.12, f32[4,292,292]{1,2,0:T(8,128)S(1)} %fusion.290, f32[4,292,292]{1,2,0:T(8,128)} %get-tuple-element.288, f32[4,292]{1,0:T(4,128)S(1)} %get-tuple-element.289), kind=kOutput, calls=%fused_computation.13.clone.1 | convolution fusion | flops 46118772 | bytes 3032128 | tf_op jit(solution)/shard_map/while/body/eval_jaxpr/pvu,pud->pvd/dot_general | solution.py:26
  55.3 2.0 convolution_convert_fusion.15
  62.5 1.9 convolution_convert_fusion.13
  69.6 1.6 convolution_convert_fusion.12
  71.2 3.1 %fusion.288 = (f32[4,292]{1,0:T(4,128)S(1)}, f32[4,292,292]{1,2,0:T(8,128)}) fusion(pred[292]{0:T(512)(128)(4,1)S(1)} %broadcast_compare_fusion.2, bf16[4,292,64]{1,2,0:T(8,128)(2,1)} %convolution_convert_fusion.12, bf16[64,64]{1,0:T(8,128)(2,1)S(1)} %copy-done.17, f32[64]{0:T(128)} %get-tuple-element.425, f32[4,292]{1,0:T(4,128)S(1)} %add_rsqrt_fusion.2, ...), kind=kOutput, calls=%fused_computation.193.clone.1 | convolution fusion | flops 55036452 | bytes 1744452 | tf_op jit(solution)/shard_map/while/body/eval_jaxpr/sub | solution.py:79
  74.3 3.5 %fusion.293 = bf16[4,292,64]{1,2,0:T(8,128)(2,1)} fusion(f32[4,292,292]{1,2,0:T(8,128)S(1)} %fusion.290, f32[4,292,292]{1,2,0:T(8,128)} %get-tuple-element.288, f32[4,292]{1,0:T(4,128)S(1)} %get-tuple-element.289, bf16[64,64]{1,0:T(8,128)(2,1)S(1)} %copy-done.17, f32[64]{0:T(128)} %get-tuple-element.425, f32[4,292]{1,0:T(4,128)S(1)} %add_rsqrt_fusion.2, ...), kind=kOutput, calls=%fused_computation.14.clone.1 | convolution fusion | flops 56135540 | bytes 7662592 | tf_op jit(solution)/shard_map/while/body/eval_jaxpr/pvu,pvd->pud/dot_general | solution.py:26
  77.9 3.5 %fusion.291 = bf16[4,292,64]{1,2,0:T(8,128)(2,1)} fusion(bf16[4,292,64]{1,2,0:T(8,128)(2,1)} %convolution_convert_fusion.12, f32[4,292,292]{1,2,0:T(8,128)S(1)} %fusion.290, f32[4,292,292]{1,2,0:T(8,128)} %get-tuple-element.288, f32[4,292]{1,0:T(4,128)S(1)} %get-tuple-element.289), kind=kOutput, calls=%fused_computation.13.clone.1 | convolution fusion | flops 46118772 | bytes 3032128 | tf_op jit(solution)/shard_map/while/body/eval_jaxpr/pvu,pud->pvd/dot_general | solution.py:26
  83.6 2.0 convolution_convert_fusion.15
  90.8 1.9 convolution_convert_fusion.13
  94.8 1.6 copy.97
  97.8 5.2 %all-to-all-start.1 = ((bf16[4,2,18688]{2,1,0:T(2,128)(2,1)}), bf16[4,2,18688]{2,1,0:T(2,128)(2,1)S(1)}, u32[]{:S(2)}, u32[]{:S(2)}) async-start(bf16[4,2,18688]{2,1,0:T(2,128)(2,1)} %reshape.106), calls=%async_computation.1 | async-start | bytes 598016 | tf_op jit(solution)/shard_map/all_to_all | solution.py:142
  106.3 6.2 %all-to-all-done.1 = bf16[4,2,18688]{2,1,0:T(2,128)(2,1)S(1)} async-done(((bf16[4,2,18688]{2,1,0:T(2,128)(2,1)}), bf16[4,2,18688]{2,1,0:T(2,128)(2,1)S(1)}, u32[]{:S(2)}, u32[]{:S(2)}) %all-to-all-start.1) | async-done | bytes 299040 | tf_op jit(solution)/shard_map/all_to_all | solution.py:142
  118.7 4.0 %collective-permute-start.2 = (bf16[64,73,1,16]{1,0,3,2:T(8,128)(2,1)S(1)}, bf16[64,73,1,16]{1,0,3,2:T(8,128)(2,1)S(1)}, u32[]{:S(2)}, u32[]{:S(2)}) collective-permute-start(bf16[64,73,1,16]{1,0,3,2:T(8,128)(2,1)S(1)} %get-tuple-element.172), channel_id=1, source_target_pairs={{0,1},{1,2},{2,3},{4,5},{5,6},{6,7},{8,9},{9,10},{10,11},{12,13},{... | collective-permute-start | bytes 448520 | tf_op jit(solution)/shard_map/ppermute | solution.py:16
  127.6 71.4 %all-reduce.8.cloned.1.call-done = (f32[64]{0:T(128)}, f32[64,64]{1,0:T(8,128)}, f32[64,64]{1,0:T(8,128)}, f32[64,64]{1,0:T(8,128)}, f32[64,64]{1,0:T(8,128)}) async-done(((f32[64]{0:T(128)}, f32[64,64]{1,0:T(8,128)}, f32[64,64]{1,0:T(8,128)}, f32[64,64]{1,0:T(8,128)}, f32[64,64]{1,0:T(8,128)}), (f32[64]{0:T(128)}, f32[64,64]{1,0:T(8,128)}, f32[64,64]{1,0:T(8,128)}, f32[64,64]{1,0:T(8,128)}, ...) | async-done | bytes 65808 | tf_op jit(solution)/shard_map/psum | solution.py:155
  199.0 97.0 %all-reduce.6.cloned.1.call-done = f32[64,64,3,3]{1,0,3,2:T(8,128)} async-done(((f32[64,64,3,3]{1,0,3,2:T(8,128)}), f32[64,64,3,3]{1,0,3,2:T(8,128)}) %all-reduce.6.cloned.1.call-update) | async-done | bytes 147472 | tf_op jit(solution)/shard_map/psum | solution.py:155
  296.0 1.7 copy.226
  (251 shorter events, 54.5 us)
Async XLA Ops:
  8.4 4.1 %collective-permute-start = (bf16[64,73,1,16]{1,0,3,2:T(8,128)(2,1)S(1)}, bf16[64,73,1,16]{1,0,3,2:T(8,128)(2,1)S(1)}, u32[]{:S(2)}, u32[]{:S(2)}) collective-permute-start(bf16[64,73,1,16]{1,0,3,2:T(8,128)(2,1)S(1)} %copy.172), channel_id=1, source_target_pairs={{0,1},{1,2},{2,3},{4,5},{5,6},{6,7},{8,9},{9,10},{10,11},{12,13},{... | collective-permute-start | bytes 448520 | tf_op jit(solution)/shard_map/ppermute | solution.py:16
  10.9 5.5 %collective-permute-start.1 = (bf16[64,73,1,16]{1,0,3,2:T(8,128)(2,1)S(1)}, bf16[64,73,1,16]{1,0,3,2:T(8,128)(2,1)S(1)}, u32[]{:S(2)}, u32[]{:S(2)}) collective-permute-start(bf16[64,73,1,16]{1,0,3,2:T(8,128)(2,1)S(1)} %copy.173), channel_id=1, source_target_pairs={{1,0},{2,1},{3,2},{5,4},{6,5},{7,6},{9,8},{10,9},{11,10},{13,12},{... | collective-permute-start | bytes 448520 | tf_op jit(solution)/shard_map/ppermute | solution.py:18
  19.1 5.9 %copy-start.18 = (bf16[64,292,2,4]{1,3,2,0:T(4,128)(2,1)S(1)}, bf16[64,292,2,4]{1,3,2,0:T(4,128)(2,1)}, u32[]{:S(2)}) copy-start(bf16[64,292,2,4]{1,3,2,0:T(4,128)(2,1)} %param.12) | copy-start | bytes 897028
  20.0 18.2 %copy-start.12 = (bf16[64,64]{1,0:T(8,128)(2,1)S(1)}, bf16[64,64]{1,0:T(8,128)(2,1)}, u32[]{:S(2)}) copy-start(bf16[64,64]{1,0:T(8,128)(2,1)} %param.19) | copy-start | bytes 24580
  20.0 18.2 %copy-start.15 = (bf16[64,64]{1,0:T(8,128)(2,1)S(1)}, bf16[64,64]{1,0:T(8,128)(2,1)}, u32[]{:S(2)}) copy-start(bf16[64,64]{1,0:T(8,128)(2,1)} %param.18) | copy-start | bytes 24580
  20.0 18.2 %copy-start.34 = (f32[64]{0:T(128)S(1)}, f32[64]{0:T(128)}, u32[]{:S(2)}) copy-start(f32[64]{0:T(128)} %param.15) | copy-start | bytes 772
  20.0 17.4 %all-to-all-start = ((bf16[64,73,2,4,4]{1,0,4,2,3:T(8,128)(2,1)}), bf16[64,73,2,4,4]{1,0,4,2,3:T(8,128)(2,1)S(1)}, u32[]{:S(2)}, u32[]{:S(2)}) async-start(bf16[64,73,2,4,4]{1,0,4,2,3:T(8,128)(2,1)} %copy.93), calls=%async_computation | async-start | bytes 1048576 | tf_op jit(solution)/shard_map/all_to_all | solution.py:131
  46.0 9.2 %copy-start.42 = (f32[4,292]{1,0:T(4,128)}, f32[4,292]{1,0:T(4,128)S(1)}, u32[]{:S(2)}) copy-start(f32[4,292]{1,0:T(4,128)S(1)} %get-tuple-element.289) | copy-start | bytes 14020 | tf_op jit(solution)/shard_map/while
  57.4 5.1 %copy-start.5 = (bf16[4,292,64]{1,2,0:T(8,128)(2,1)S(1)}, bf16[4,292,64]{1,2,0:T(8,128)(2,1)}, u32[]{:S(2)}) copy-start(bf16[4,292,64]{1,2,0:T(8,128)(2,1)} %copy-done.4) | copy-start | bytes 448516 | tf_op jit(solution)/shard_map/while
  57.4 5.1 %copy-start.43 = (f32[4,292]{1,0:T(4,128)S(1)}, f32[4,292]{1,0:T(4,128)}, u32[]{:S(2)}) copy-start(f32[4,292]{1,0:T(4,128)} %copy-done.42) | copy-start | bytes 14020 | tf_op jit(solution)/shard_map/while
  74.3 9.2 %copy-start.42 = (f32[4,292]{1,0:T(4,128)}, f32[4,292]{1,0:T(4,128)S(1)}, u32[]{:S(2)}) copy-start(f32[4,292]{1,0:T(4,128)S(1)} %get-tuple-element.289) | copy-start | bytes 14020 | tf_op jit(solution)/shard_map/while
  85.7 5.1 %copy-start.5 = (bf16[4,292,64]{1,2,0:T(8,128)(2,1)S(1)}, bf16[4,292,64]{1,2,0:T(8,128)(2,1)}, u32[]{:S(2)}) copy-start(bf16[4,292,64]{1,2,0:T(8,128)(2,1)} %copy-done.4) | copy-start | bytes 448516 | tf_op jit(solution)/shard_map/while
  85.7 5.1 %copy-start.43 = (f32[4,292]{1,0:T(4,128)S(1)}, f32[4,292]{1,0:T(4,128)}, u32[]{:S(2)}) copy-start(f32[4,292]{1,0:T(4,128)} %copy-done.42) | copy-start | bytes 14020 | tf_op jit(solution)/shard_map/while
  94.8 8.2 %copy-start.27 = (f32[2,64,64]{2,1,0:T(8,128)S(1)}, f32[2,64,64]{2,1,0:T(8,128)}, u32[]{:S(2)}) copy-start(f32[2,64,64]{2,1,0:T(8,128)} %get-tuple-element.410) | copy-start | bytes 98308
  94.8 8.8 %copy-start.30 = (f32[2,64,64]{2,1,0:T(8,128)S(1)}, f32[2,64,64]{2,1,0:T(8,128)}, u32[]{:S(2)}) copy-start(f32[2,64,64]{2,1,0:T(8,128)} %get-tuple-element.411) | copy-start | bytes 98308
  94.8 9.4 %copy-start.33 = (f32[2,64,64]{2,1,0:T(8,128)S(1)}, f32[2,64,64]{2,1,0:T(8,128)}, u32[]{:S(2)}) copy-start(f32[2,64,64]{2,1,0:T(8,128)} %get-tuple-element.412) | copy-start | bytes 98308
  94.8 10.1 %copy-start.24 = (f32[2,64,64]{2,1,0:T(8,128)S(1)}, f32[2,64,64]{2,1,0:T(8,128)}, u32[]{:S(2)}) copy-start(f32[2,64,64]{2,1,0:T(8,128)} %get-tuple-element.413) | copy-start | bytes 98308
  94.8 10.7 %copy-start.39 = (f32[2,64]{1,0:T(2,128)S(1)}, f32[2,64]{1,0:T(2,128)}, u32[]{:S(2)}) copy-start(f32[2,64]{1,0:T(2,128)} %get-tuple-element.409) | copy-start | bytes 1540
  97.8 14.7 %all-to-all-start.1 = ((bf16[4,2,18688]{2,1,0:T(2,128)(2,1)}), bf16[4,2,18688]{2,1,0:T(2,128)(2,1)S(1)}, u32[]{:S(2)}, u32[]{:S(2)}) async-start(bf16[4,2,18688]{2,1,0:T(2,128)(2,1)} %reshape.106), calls=%async_computation.1 | async-start | bytes 598016 | tf_op jit(solution)/shard_map/all_to_all | solution.py:142
  103.0 96.1 %all-reduce.8.cloned.1.call-start = ((), (), s32[]{:S(2)}) async-start(), calls=%async_computation.3 | async-start | bytes 263168 | tf_op jit(solution)/shard_map/psum | solution.py:155
  106.0 190.0 %all-reduce.6.cloned.1.call-start = ((), (), s32[]{:S(2)}) async-start(), calls=%async_computation.2 | async-start | bytes 589824 | tf_op jit(solution)/shard_map/psum | solution.py:155
  117.4 5.3 %copy-start.21 = (f32[64,64,9]{1,0,2:T(8,128)}, f32[64,64,9]{1,0,2:T(8,128)S(1)}, u32[]{:S(2)}) copy-start(f32[64,64,9]{1,0,2:T(8,128)S(1)} %fusion.104) | copy-start | bytes 442372
  117.4 5.6 %collective-permute-start.3 = (bf16[64,73,1,16]{1,0,3,2:T(8,128)(2,1)S(1)}, bf16[64,73,1,16]{1,0,3,2:T(8,128)(2,1)S(1)}, u32[]{:S(2)}, u32[]{:S(2)}) collective-permute-start(bf16[64,73,1,16]{1,0,3,2:T(8,128)(2,1)S(1)} %get-tuple-element.173), channel_id=1, source_target_pairs={{1,0},{2,1},{3,2},{5,4},{6,5},{7,6},{9,8},{10,9},{11,10},{13,12},{... | collective-permute-start | bytes 448520 | tf_op jit(solution)/shard_map/ppermute | solution.py:18
  118.7 5.1 %collective-permute-start.2 = (bf16[64,73,1,16]{1,0,3,2:T(8,128)(2,1)S(1)}, bf16[64,73,1,16]{1,0,3,2:T(8,128)(2,1)S(1)}, u32[]{:S(2)}, u32[]{:S(2)}) collective-permute-start(bf16[64,73,1,16]{1,0,3,2:T(8,128)(2,1)S(1)} %get-tuple-element.172), channel_id=1, source_target_pairs={{0,1},{1,2},{2,3},{4,5},{5,6},{6,7},{8,9},{9,10},{10,11},{12,13},{... | collective-permute-start | bytes 448520 | tf_op jit(solution)/shard_map/ppermute | solution.py:16
  (55 other events, 161.9 us)
Sparse Core Ops, SparseCore 0:
  108.4 90.5 all-reduce.7
  203.0 93.0 all-reduce.5
where the time goes:
time: 313 us; the launch traced here: 311 us
  waiting for transfers between devices  191 us (61%)
  matrix products  58.5 us (19%)
  local copies, waits for them, and re-layouts  22.2 us (7%)
  starting transfers between devices  19.4 us (6%)
  between operations  14.6 us (5%)
  other arithmetic  5.07 us (2%)
    psum x2, waiting for transfers between devices, body(): lax.psum((g_conv, g_gain, g_query, g_key, g_value, g_out), ('view', 'row'))  168 us
    dot_general x59, matrix products, product(): return jnp.einsum(form, left, right, preferred_element_type=jnp.float32)  52.2 us
    unnamed x48, local copies, waits for them, and re-layouts  12.6 us
    all_to_all x1, waiting for transfers between devices, body(): lax.all_to_all(spatial.reshape(channels, view_dev, row_dev, blocks, bread...  12.3 us
    ppermute x2, starting transfers between devices, with_halo(): lax.ppermute(tail, axis, [(i, (i + 1) % count) for i in range(ends)])  6.37 us
  transfers between devices with their start and end apart: 8, of which 6 were waited for; matrix products, arithmetic and copies ran while one was open for 4% of the time, Pallas kernels for 0%

commit v1 on v0

--- a/solution.py
+++ b/solution.py
@@ -3,6 +3,27 @@
 import jax.numpy as jnp
 from jax import lax
 from jax.sharding import PartitionSpec as P
+
+
+def _bind_words(block_here):
+    x_next = lax.axis_size("view")
+    part_now = lax.axis_index("view")
+    known, b_next = (x_next, part_now)
+    near = block_here.shape[3] // known
+    q_next = list(block_here.shape)
+    q_next[3] = near
+    front = q_next[1]
+    q_next[1] = front * known
+    out_arr = jnp.zeros(q_next, block_here.dtype)
+    for b in range(known):
+        p_next = lax.dynamic_slice_in_dim(block_here, (b_next ^ b) * near, near, axis=3)
+        if b:
+            row_list = []
+            for dev_j in range(known):
+                row_list.append((dev_j, dev_j ^ b))
+            p_next = lax.ppermute(p_next, "view", row_list)
+        out_arr = lax.dynamic_update_slice_in_dim(out_arr, p_next, (b_next ^ b) * front, axis=1)
+    return out_arr
 
 
 def with_halo(cells, sides, width):
@@ -128,13 +149,7 @@
     padded = with_halo(inputs, (("row", 2),), 1)
     padded = jnp.pad(padded, ((0, 0), (0, 0), (0, 0), (1, 1)))
     spatial = (inputs.astype(jnp.float32) + convolve(padded, w_conv)).astype(jnp.bfloat16)
-    moved = lax.all_to_all(
-        spatial.reshape(channels, view_dev, row_dev, blocks, breadth),
-        "view",
-        split_axis=3,
-        concat_axis=1,
-        tiled=True,
-    )
+    moved = _bind_words(spatial.reshape(channels, view_dev, row_dev, blocks, breadth))
     moved = moved.reshape(channels, all_views, row_dev, breadth)
     output, d_spatial, grads = angular_rows(
         moved, cotangent, keep, gain, w_query, w_key, w_value, w_out, all_views

time: 313 us -> 301 us (0.962)
  waiting for transfers between devices: 191 us -> 182 us
  matrix products: 58.5 us -> 52.7 us
  local copies, waits for them, and re-layouts: 22.2 us -> 25.7 us
    all_to_all x1 -> x0, waiting for transfers between devices: 12.3 us -> none  [body(): lax.all_to_all(spatial.reshape(channels, view_dev, row_dev, blocks, bread...]
    dynamic_update_slice x0 -> x4, local copies, waits for them, and re-layouts: none -> 6.17 us  [_bind_words(): lax.dynamic_update_slice_in_dim(out_arr, p_next, (b_next ^ b) * front, ax...]
    dot_general x59, matrix products: 52.2 us -> 46.5 us  [product(): return jnp.einsum(form, left, right, preferred_element_type=jnp.float32)]
    all_to_all x1 -> x0, starting transfers between devices: 5 us -> none  [body(): lax.all_to_all(spatial.reshape(channels, view_dev, row_dev, blocks, bread...]
    ppermute x0 -> x3, starting transfers between devices: none -> 4.45 us  [_bind_words(): p_next = lax.ppermute(p_next, 'view', row_list)]
    ppermute x0 -> x3, waiting for transfers between devices: none -> 3.51 us  [_bind_words(): p_next = lax.ppermute(p_next, 'view', row_list)]
    unnamed x48 -> x51, local copies, waits for them, and re-layouts: 12.6 us -> 12.6 us
  transfers between devices with their start and end apart: 8 -> 10, of which waited for: 6 -> 7; matrix products, arithmetic and copies ran while one was open for 4% -> 6% of each run, Pallas kernels for 0% -> 0%
where the time goes in v1:
time: 301 us; the launch traced here: 300 us
  waiting for transfers between devices  182 us (60%)
  matrix products  52.7 us (18%)
  local copies, waits for them, and re-layouts  25.7 us (9%)
  starting transfers between devices  19.9 us (7%)
  between operations  14.7 us (5%)
  other arithmetic  4.59 us (2%)
    psum x2, waiting for transfers between devices, body(): lax.psum((g_conv, g_gain, g_query, g_key, g_value, g_out), ('view', 'row'))  169 us
    dot_general x59, matrix products, product(): return jnp.einsum(form, left, right, preferred_element_type=jnp.float32)  46.5 us
    unnamed x51, local copies, waits for them, and re-layouts  12.6 us
    ppermute x2, starting transfers between devices, with_halo(): lax.ppermute(tail, axis, [(i, (i + 1) % count) for i in range(ends)])  6.8 us
    sub x2, matrix products, angular(): expo = jnp.exp(scores - highest)  6.21 us
    dynamic_update_slice x4, local copies, waits for them, and re-layouts, _bind_words(): lax.dynamic_update_slice_in_dim(out_arr, p_next, (b_next ^ b) * front, ax...  6.17 us
  transfers between devices with their start and end apart: 10, of which 7 were waited for; matrix products, arithmetic and copies ran while one was open for 6% of the time, Pallas kernels for 0%

profile of v1, /device:TPU:0, one launch (start us, length us, event | category | flops | bytes accessed | tf_op | source)
XLA Modules:
  0.0 299.8 jit_solution(4222755778860136603)
XLA Ops:
  8.4 2.4 collective-permute-start
  13.2 3.2 %collective-permute-done.1 = bf16[64,73,1,16]{1,0,3,2:T(8,128)(2,1)S(1)} collective-permute-done((bf16[64,73,1,16]{1,0,3,2:T(8,128)(2,1)S(1)}, bf16[64,73,1,16]{1,0,3,2:T(8,128)(2,1)S(1)}, u32[]{:S(2)}, u32[]{:S(2)}) %collective-permute-start.1) | collective-permute-done | bytes 149536 | tf_op jit(solution)/shard_map/ppermute | solution.py:39
  20.9 2.6 collective-permute-start.3
  24.6 1.8 dynamic_update_slice.41
  26.4 1.8 collective-permute-done.3
  28.2 1.8 dynamic_update_slice.42
  31.7 1.8 dynamic_update_slice.43
  33.6 48.1 %while.22 = (s32[]{:T(128)}, bf16[2,4,292,64]{2,1,0,3:T(4,128)(2,1)}, bf16[2,4,292,64]{2,3,1,0:T(8,128)(2,1)}, f32[2,64]{1,0:T(2,128)S(1)}, f32[2,64,64]{2,1,0:T...) while((s32[]{:T(128)}, ...), condition=%wide.region_9.10_spmd, body=%wide.region_0.9_spmd.sunk | while | flops 399432576 | bytes 35000580 | solution.py:139
  37.7 3.1 %fusion.288 = (f32[4,292]{1,0:T(4,128)S(1)}, f32[4,292,292]{1,2,0:T(8,128)}) fusion(pred[292]{0:T(512)(128)(4,1)S(1)} %broadcast_compare_fusion.2, bf16[4,292,64]{1,2,0:T(8,128)(2,1)} %convolution_convert_fusion.12, bf16[64,64]{1,0:T(8,128)(2,1)S(1)} %get-tuple-element.339, f32[64]{0:T(128)S(1)} %get-tuple-element.338, ...), kind=kOutput, calls=%fused_computation.197.clone.1 | convolution fusion | flops 55036452 | bytes 1744708 | tf_op jit(solution)/shard_map/while/body/eval_jaxpr/sub | solution.py:100
  40.8 3.5 %fusion.293 = bf16[4,292,64]{1,2,0:T(8,128)(2,1)} fusion(f32[4,292,292]{1,2,0:T(8,128)S(1)} %fusion.290, f32[4,292,292]{1,2,0:T(8,128)} %get-tuple-element.284, f32[4,292]{1,0:T(4,128)S(1)} %get-tuple-element.285, bf16[64,64]{1,0:T(8,128)(2,1)S(1)} %get-tuple-element.339, f32[64]{0:T(128)S(1)} %get-tuple-element.338, ...), kind=kOutput, calls=%fused_computation.14.clone.1 | convolution fusion | flops 56135540 | bytes 7662592 | tf_op jit(solution)/shard_map/while/body/eval_jaxpr/pvu,pvd->pud/dot_general | solution.py:47
  44.3 3.5 %fusion.291 = bf16[4,292,64]{1,2,0:T(8,128)(2,1)} fusion(bf16[4,292,64]{1,2,0:T(8,128)(2,1)} %convolution_convert_fusion.12, f32[4,292,292]{1,2,0:T(8,128)S(1)} %fusion.290, f32[4,292,292]{1,2,0:T(8,128)} %get-tuple-element.284, f32[4,292]{1,0:T(4,128)S(1)} %get-tuple-element.285), kind=kOutput, calls=%fused_computation.13.clone.1 | convolution fusion | flops 46118772 | bytes 3032128 | tf_op jit(solution)/shard_map/while/body/eval_jaxpr/pvu,pud->pvd/dot_general | solution.py:47
  50.0 2.0 convolution_convert_fusion.15
  54.4 1.9 convolution_convert_fusion.13
  61.7 3.1 %fusion.288 = (f32[4,292]{1,0:T(4,128)S(1)}, f32[4,292,292]{1,2,0:T(8,128)}) fusion(pred[292]{0:T(512)(128)(4,1)S(1)} %broadcast_compare_fusion.2, bf16[4,292,64]{1,2,0:T(8,128)(2,1)} %convolution_convert_fusion.12, bf16[64,64]{1,0:T(8,128)(2,1)S(1)} %get-tuple-element.339, f32[64]{0:T(128)S(1)} %get-tuple-element.338, ...), kind=kOutput, calls=%fused_computation.197.clone.1 | convolution fusion | flops 55036452 | bytes 1744708 | tf_op jit(solution)/shard_map/while/body/eval_jaxpr/sub | solution.py:100
  64.8 3.5 %fusion.293 = bf16[4,292,64]{1,2,0:T(8,128)(2,1)} fusion(f32[4,292,292]{1,2,0:T(8,128)S(1)} %fusion.290, f32[4,292,292]{1,2,0:T(8,128)} %get-tuple-element.284, f32[4,292]{1,0:T(4,128)S(1)} %get-tuple-element.285, bf16[64,64]{1,0:T(8,128)(2,1)S(1)} %get-tuple-element.339, f32[64]{0:T(128)S(1)} %get-tuple-element.338, ...), kind=kOutput, calls=%fused_computation.14.clone.1 | convolution fusion | flops 56135540 | bytes 7662592 | tf_op jit(solution)/shard_map/while/body/eval_jaxpr/pvu,pvd->pud/dot_general | solution.py:47
  68.3 3.5 %fusion.291 = bf16[4,292,64]{1,2,0:T(8,128)(2,1)} fusion(bf16[4,292,64]{1,2,0:T(8,128)(2,1)} %convolution_convert_fusion.12, f32[4,292,292]{1,2,0:T(8,128)S(1)} %fusion.290, f32[4,292,292]{1,2,0:T(8,128)} %get-tuple-element.284, f32[4,292]{1,0:T(4,128)S(1)} %get-tuple-element.285), kind=kOutput, calls=%fused_computation.13.clone.1 | convolution fusion | flops 46118772 | bytes 3032128 | tf_op jit(solution)/shard_map/while/body/eval_jaxpr/pvu,pud->pvd/dot_general | solution.py:47
  74.1 2.0 convolution_convert_fusion.15
  78.5 1.9 convolution_convert_fusion.13
  84.6 6.0 %all-to-all-start = ((bf16[4,2,18688]{2,1,0:T(2,128)(2,1)}), bf16[4,2,18688]{2,1,0:T(2,128)(2,1)S(1)}, u32[]{:S(2)}, u32[]{:S(2)}) async-start(bf16[4,2,18688]{2,1,0:T(2,128)(2,1)} %reshape.125), calls=%async_computation | async-start | bytes 598016 | tf_op jit(solution)/shard_map/all_to_all | solution.py:157
  94.5 5.4 %all-to-all-done = bf16[4,2,18688]{2,1,0:T(2,128)(2,1)S(1)} async-done(((bf16[4,2,18688]{2,1,0:T(2,128)(2,1)}), bf16[4,2,18688]{2,1,0:T(2,128)(2,1)S(1)}, u32[]{:S(2)}, u32[]{:S(2)}) %all-to-all-start) | async-done | bytes 299040 | tf_op jit(solution)/shard_map/all_to_all | solution.py:157
  106.1 4.4 %collective-permute-start.5 = (bf16[64,73,1,16]{1,0,3,2:T(8,128)(2,1)S(1)}, bf16[64,73,1,16]{1,0,3,2:T(8,128)(2,1)S(1)}, u32[]{:S(2)}, u32[]{:S(2)}) collective-permute-start(bf16[64,73,1,16]{1,0,3,2:T(8,128)(2,1)S(1)} %get-tuple-element.164), channel_id=1, source_target_pairs={{0,1},{1,2},{2,3},{4,5},{5,6},{6,7},{8,9},{9,10},{10,11},{12,13},{... | collective-permute-start | bytes 448520 | tf_op jit(solution)/shard_map/ppermute | solution.py:37
  115.3 72.4 %all-reduce.8.cloned.1.call-done = (f32[64]{0:T(128)}, f32[64,64]{1,0:T(8,128)}, f32[64,64]{1,0:T(8,128)}, f32[64,64]{1,0:T(8,128)}, f32[64,64]{1,0:T(8,128)}) async-done(((f32[64]{0:T(128)}, f32[64,64]{1,0:T(8,128)}, f32[64,64]{1,0:T(8,128)}, f32[64,64]{1,0:T(8,128)}, f32[64,64]{1,0:T(8,128)}), (f32[64]{0:T(128)}, f32[64,64]{1,0:T(8,128)}, f32[64,64]{1,0:T(8,128)}, f32[64,64]{1,0:T(8,128)}, ...) | async-done | bytes 65808 | tf_op jit(solution)/shard_map/psum | solution.py:170
  187.6 97.0 %all-reduce.6.cloned.1.call-done = f32[64,64,3,3]{1,0,3,2:T(8,128)} async-done(((f32[64,64,3,3]{1,0,3,2:T(8,128)}), f32[64,64,3,3]{1,0,3,2:T(8,128)}) %all-reduce.6.cloned.1.call-update) | async-done | bytes 147472 | tf_op jit(solution)/shard_map/psum | solution.py:170
  284.6 1.7 copy.205
  (216 shorter events, 54.3 us)
Async XLA Ops:
  7.2 5.1 %copy-start.2 = (bf16[64,73,2,16]{1,3,2,0:T(8,128)(2,1)S(1)}, bf16[64,73,2,16]{1,3,2,0:T(8,128)(2,1)}, u32[]{:S(2)}) copy-start(bf16[64,73,2,16]{1,3,2,0:T(8,128)(2,1)} %param.11) | copy-start | bytes 897028
  7.2 5.1 %copy-start.13 = (bf16[64,64,3,3]{1,0,3,2:T(8,128)(2,1)S(1)}, bf16[64,64,3,3]{1,0,3,2:T(8,128)(2,1)}, u32[]{:S(2)}) copy-start(bf16[64,64,3,3]{1,0,3,2:T(8,128)(2,1)} %param.14) | copy-start | bytes 221188
  8.4 4.2 %collective-permute-start = (bf16[64,73,1,16]{1,0,3,2:T(8,128)(2,1)S(1)}, bf16[64,73,1,16]{1,0,3,2:T(8,128)(2,1)S(1)}, u32[]{:S(2)}, u32[]{:S(2)}) collective-permute-start(bf16[64,73,1,16]{1,0,3,2:T(8,128)(2,1)S(1)} %copy.147), channel_id=1, source_target_pairs={{0,1},{1,2},{2,3},{4,5},{5,6},{6,7},{8,9},{9,10},{10,11},{12,13},{... | collective-permute-start | bytes 448520 | tf_op jit(solution)/shard_map/ppermute | solution.py:37
  10.9 5.5 %collective-permute-start.1 = (bf16[64,73,1,16]{1,0,3,2:T(8,128)(2,1)S(1)}, bf16[64,73,1,16]{1,0,3,2:T(8,128)(2,1)S(1)}, u32[]{:S(2)}, u32[]{:S(2)}) collective-permute-start(bf16[64,73,1,16]{1,0,3,2:T(8,128)(2,1)S(1)} %copy.148), channel_id=1, source_target_pairs={{1,0},{2,1},{3,2},{5,4},{6,5},{7,6},{9,8},{10,9},{11,10},{13,12},{... | collective-permute-start | bytes 448520 | tf_op jit(solution)/shard_map/ppermute | solution.py:39
  18.6 5.1 %copy-start.17 = (bf16[64,292,2,4]{1,3,2,0:T(4,128)(2,1)S(1)}, bf16[64,292,2,4]{1,3,2,0:T(4,128)(2,1)}, u32[]{:S(2)}) copy-start(bf16[64,292,2,4]{1,3,2,0:T(4,128)(2,1)} %param.12) | copy-start | bytes 897028
  19.1 14.4 %copy-start.12 = (bf16[64,64]{1,0:T(8,128)(2,1)S(1)}, bf16[64,64]{1,0:T(8,128)(2,1)}, u32[]{:S(2)}) copy-start(bf16[64,64]{1,0:T(8,128)(2,1)} %param.19) | copy-start | bytes 24580
  19.1 14.4 %copy-start.14 = (bf16[64,64]{1,0:T(8,128)(2,1)S(1)}, bf16[64,64]{1,0:T(8,128)(2,1)}, u32[]{:S(2)}) copy-start(bf16[64,64]{1,0:T(8,128)(2,1)} %param.17) | copy-start | bytes 24580
  19.1 14.4 %copy-start.15 = (bf16[64,64]{1,0:T(8,128)(2,1)S(1)}, bf16[64,64]{1,0:T(8,128)(2,1)}, u32[]{:S(2)}) copy-start(bf16[64,64]{1,0:T(8,128)(2,1)} %param.18) | copy-start | bytes 24580
  19.1 14.4 %copy-start.16 = (bf16[64,64]{1,0:T(8,128)(2,1)S(1)}, bf16[64,64]{1,0:T(8,128)(2,1)}, u32[]{:S(2)}) copy-start(bf16[64,64]{1,0:T(8,128)(2,1)} %param.16) | copy-start | bytes 24580
  19.2 14.4 %copy-start.30 = (f32[64]{0:T(128)S(1)}, f32[64]{0:T(128)}, u32[]{:S(2)}) copy-start(f32[64]{0:T(128)} %param.15) | copy-start | bytes 772
  19.2 14.4 %copy-start.31 = (s32[292]{0:T(512)S(1)}, s32[292]{0:T(512)}, u32[]{:S(2)}) copy-start(s32[292]{0:T(512)} %param.13) | copy-start | bytes 3508
  19.2 5.3 %collective-permute-start.2 = (bf16[64,73,2,1,4]{1,0,4,2,3:T(8,128)(2,1)S(1)}, bf16[64,73,2,1,4]{1,0,4,2,3:T(8,128)(2,1)S(1)}, u32[]{:S(2)}, u32[]{:S(2)}) collective-permute-start(bf16[64,73,2,1,4]{1,0,4,2,3:T(8,128)(2,1)S(1)} %get-tuple-element.168), channel_id=1, source_target_pairs={{0,4},{4,0},{8,12},{12,8},{1,5},{5,1},{9,13},{13,9},{2,6},{6,2},{1... | collective-permute-start | bytes 224264 | tf_op jit(solution)/shard_map/ppermute | solution.py:24
  20.9 7.4 %collective-permute-start.3 = (bf16[64,73,2,1,4]{1,0,4,2,3:T(8,128)(2,1)S(1)}, bf16[64,73,2,1,4]{1,0,4,2,3:T(8,128)(2,1)S(1)}, u32[]{:S(2)}, u32[]{:S(2)}) collective-permute-start(bf16[64,73,2,1,4]{1,0,4,2,3:T(8,128)(2,1)S(1)} %get-tuple-element.167), channel_id=1, source_target_pairs={{0,8},{4,12},{8,0},{12,4},{1,9},{5,13},{9,1},{13,5},{2,10},{6,14},... | collective-permute-start | bytes 224264 | tf_op jit(solution)/shard_map/ppermute | solution.py:24
  23.5 8.3 %collective-permute-start.4 = (bf16[64,73,2,1,4]{1,0,4,2,3:T(8,128)(2,1)S(1)}, bf16[64,73,2,1,4]{1,0,4,2,3:T(8,128)(2,1)S(1)}, u32[]{:S(2)}, u32[]{:S(2)}) collective-permute-start(bf16[64,73,2,1,4]{1,0,4,2,3:T(8,128)(2,1)S(1)} %get-tuple-element.166), channel_id=1, source_target_pairs={{0,12},{4,8},{8,4},{12,0},{1,13},{5,9},{9,5},{13,1},{2,14},{6,10},... | collective-permute-start | bytes 224264 | tf_op jit(solution)/shard_map/ppermute | solution.py:24
  52.7 4.3 %copy-start.19 = (bf16[2,4,292,64]{2,3,1,0:T(8,128)(2,1)}, bf16[2,4,292,64]{2,3,1,0:T(8,128)(2,1)S(1)}, u32[]{:S(2)}) copy-start(bf16[2,4,292,64]{2,3,1,0:T(8,128)(2,1)S(1)} %fusion.295) | copy-start | bytes 897028 | tf_op jit(solution)/shard_map/while
  81.7 8.9 %copy-start.26 = (f32[2,64,64]{2,1,0:T(8,128)S(1)}, f32[2,64,64]{2,1,0:T(8,128)}, u32[]{:S(2)}) copy-start(f32[2,64,64]{2,1,0:T(8,128)} %get-tuple-element.99) | copy-start | bytes 98308
  81.7 9.5 %copy-start.29 = (f32[2,64,64]{2,1,0:T(8,128)S(1)}, f32[2,64,64]{2,1,0:T(8,128)}, u32[]{:S(2)}) copy-start(f32[2,64,64]{2,1,0:T(8,128)} %get-tuple-element.100) | copy-start | bytes 98308
  81.7 11.6 %copy-start.23 = (f32[2,64,64]{2,1,0:T(8,128)S(1)}, f32[2,64,64]{2,1,0:T(8,128)}, u32[]{:S(2)}) copy-start(f32[2,64,64]{2,1,0:T(8,128)} %get-tuple-element.102) | copy-start | bytes 98308
  84.6 15.3 %all-to-all-start = ((bf16[4,2,18688]{2,1,0:T(2,128)(2,1)}), bf16[4,2,18688]{2,1,0:T(2,128)(2,1)S(1)}, u32[]{:S(2)}, u32[]{:S(2)}) async-start(bf16[4,2,18688]{2,1,0:T(2,128)(2,1)} %reshape.125), calls=%async_computation | async-start | bytes 598016 | tf_op jit(solution)/shard_map/all_to_all | solution.py:157
  90.6 97.0 %all-reduce.8.cloned.1.call-start = ((), (), s32[]{:S(2)}) async-start(), calls=%async_computation.2 | async-start | bytes 263168 | tf_op jit(solution)/shard_map/psum | solution.py:170
  94.5 190.1 %all-reduce.6.cloned.1.call-start = ((), (), s32[]{:S(2)}) async-start(), calls=%async_computation.1 | async-start | bytes 589824 | tf_op jit(solution)/shard_map/psum | solution.py:170
  104.8 5.7 %copy-start.20 = (f32[64,64,9]{1,0,2:T(8,128)}, f32[64,64,9]{1,0,2:T(8,128)S(1)}, u32[]{:S(2)}) copy-start(f32[64,64,9]{1,0,2:T(8,128)S(1)} %fusion.104) | copy-start | bytes 442372
  104.8 6.1 %collective-permute-start.6 = (bf16[64,73,1,16]{1,0,3,2:T(8,128)(2,1)S(1)}, bf16[64,73,1,16]{1,0,3,2:T(8,128)(2,1)S(1)}, u32[]{:S(2)}, u32[]{:S(2)}) collective-permute-start(bf16[64,73,1,16]{1,0,3,2:T(8,128)(2,1)S(1)} %get-tuple-element.165), channel_id=1, source_target_pairs={{1,0},{2,1},{3,2},{5,4},{6,5},{7,6},{9,8},{10,9},{11,10},{13,12},{... | collective-permute-start | bytes 448520 | tf_op jit(solution)/shard_map/ppermute | solution.py:39
  106.1 5.3 %collective-permute-start.5 = (bf16[64,73,1,16]{1,0,3,2:T(8,128)(2,1)S(1)}, bf16[64,73,1,16]{1,0,3,2:T(8,128)(2,1)S(1)}, u32[]{:S(2)}, u32[]{:S(2)}) collective-permute-start(bf16[64,73,1,16]{1,0,3,2:T(8,128)(2,1)S(1)} %get-tuple-element.164), channel_id=1, source_target_pairs={{0,1},{1,2},{2,3},{4,5},{5,6},{6,7},{8,9},{9,10},{10,11},{12,13},{... | collective-permute-start | bytes 448520 | tf_op jit(solution)/shard_map/ppermute | solution.py:37
  (36 other events, 63.9 us)
Sparse Core Ops, SparseCore 0:
  96.0 91.5 all-reduce.7
  191.6 93.0 all-reduce.5
